TPU v7x, 256 devices: a whole 4x4x8 slice. The times are simulated.
256 devices in a mesh: head: 8 (over y, core), tok: 32 (over x, z).
Axes of the slice: x: 4, y: 4, z: 8, core: 2. Of those that a mesh axis runs over, the one named last changes fastest.
Arguments:
- queries: bfloat16 [32768, 4096], P('tok', 'head'), may hold values from -100 to 100
- keys: bfloat16 [32768, 4096], P('tok', 'head'), may hold values from -6 to 6
- values: bfloat16 [32768, 4096], P('tok', 'head'), may hold values from -6 to 6
- step_size: float32 [32768, 8], P('tok', 'head'), may hold values from 6.1035156e-05 to 0.00061035156
- fast_one: bfloat16 [8, 512, 512], P('head'), may hold values from -0.25 to 0.25
- fast_three: bfloat16 [8, 512, 512], P('head'), may hold values from -0.25 to 0.25
- fast_two: bfloat16 [8, 512, 512], P('head'), may hold values from -0.25 to 0.25
- out_proj: bfloat16 [4096, 4096], P('tok', 'head'), may hold values from -0.09375 to 0.09375
- view_units: int32 [64], replicated, may hold values from 1 to 8, 256 in all
- evening: int32 [32, 32], P('tok'), may hold values from 0 to 31, each once within a row
Outputs:
- evened: bfloat16 [32768, 4096], P('tok', 'head')
Inputs may be any that keep to these rules, and one draw needn't show every extreme that they name: `view_units`: the lengths sum to 256; the longest is exactly 8. `evening`: each row is a permutation of the token shards.
All inputs are finite; a program needn't handle non-finite values.
Results may differ from a plain program's by a relative error of at most 0.01.
The roundings to bfloat16 on the way count: a program that leaves them out, or rounds other values in their place, can miss the bound.
Values may be sent and summed in bfloat16 or wider, within the bound.
No kernel may reach another device: no remote copies, remote signals or barrier semaphores. Data moves between devices by JAX's collectives and lax.ppermute only.
A program may use at most 64 MiB of HBM per device.

v0:
```python
import jax
import jax.numpy as jnp
from jax import lax
from jax.sharding import PartitionSpec as P

DH = 512
VIEW_UNIT = 128
VIEW_MOST = 8


def from_behind(value, axis, steps):
    count = lax.axis_size(axis)
    leading, last = (max(0, -steps), min(count, count - steps))
    return lax.ppermute(value, axis, [(source, source + steps) for source in range(leading, last)])


def view_lookup(view_units, positions, total_tokens):
    view_ends = jnp.cumsum(view_units) * VIEW_UNIT
    inside = (positions >= 0) & (positions < total_tokens)
    labels = jnp.sum((positions[:, None] >= view_ends[None, :]).astype(jnp.int32), axis=1)
    return jnp.where(inside, labels, -1)


def rms_rows(rows):
    return rows * lax.rsqrt(jnp.mean(rows * rows, axis=-1, keepdims=True) + 1e-06)


def local(
    queries, keys, values, step_size, fast_one, fast_three, fast_two, out_proj, view_units, evening
):
    shard_count = lax.axis_size("tok")
    my_shard = lax.axis_index("tok")
    tok_dev = queries.shape[0]
    local_width = queries.shape[1]
    heads_here = local_width // DH
    total_tokens = tok_dev * shard_count
    reach_span = (VIEW_MOST * VIEW_UNIT + tok_dev - 2) // tok_dev
    scale = DH ** (-0.5)
    local_rows = jnp.arange(tok_dev, dtype=jnp.int32)
    stacked = jnp.stack([keys, values])
    pieces = []
    labels = []
    offsets = list(range(reach_span, 0, -1)) + [0] + list(range(-1, -reach_span - 1, -1))
    for offset in offsets:
        if offset == 0:
            pieces.append(stacked)
        else:
            pieces.append(from_behind(stacked, "tok", offset))
        labels.append(
            view_lookup(view_units, (my_shard - offset) * tok_dev + local_rows, total_tokens)
        )
    window = jnp.concatenate(pieces, axis=1)
    key_views = jnp.concatenate(labels)
    key_heads = window[0].reshape(-1, heads_here, DH)
    value_heads = window[1].reshape(-1, heads_here, DH)
    window_rows = key_heads.shape[0]
    query_views = view_lookup(view_units, my_shard * tok_dev + local_rows, total_tokens)
    block_rows = min(512, tok_dev)
    n_blocks = tok_dev // block_rows
    key_span = min(window_rows, block_rows + 2 * VIEW_MOST * VIEW_UNIT)
    lead_shift = reach_span * tok_dev - VIEW_MOST * VIEW_UNIT

    def attend(block_index):
        start = block_index * block_rows
        key_start = jnp.clip(start + lead_shift, 0, window_rows - key_span)
        query_rows = lax.dynamic_slice_in_dim(queries, start, block_rows, 0).reshape(
            block_rows, heads_here, DH
        )
        row_views = lax.dynamic_slice_in_dim(query_views, start, block_rows, 0)
        near_keys = lax.dynamic_slice_in_dim(key_heads, key_start, key_span, 0)
        near_values = lax.dynamic_slice_in_dim(value_heads, key_start, key_span, 0)
        near_views = lax.dynamic_slice_in_dim(key_views, key_start, key_span, 0)
        scores = (
            jnp.einsum("qhd,khd->hqk", query_rows, near_keys, preferred_element_type=jnp.float32)
            * scale
        )
        same_view = row_views[:, None] == near_views[None, :]
        scores = jnp.where(same_view[None], scores, -1e30)
        top = jnp.max(scores, axis=-1, keepdims=True)
        weights = jnp.exp(scores - top)
        probs = (weights / jnp.sum(weights, axis=-1, keepdims=True)).astype(jnp.bfloat16)
        out_rows = jnp.einsum(
            "hqk,khd->qhd", probs, near_values, preferred_element_type=jnp.float32
        )
        return out_rows.reshape(block_rows, local_width)

    attended = lax.map(attend, jnp.arange(n_blocks, dtype=jnp.int32)).reshape(tok_dev, local_width)
    query_norm = rms_rows(queries.reshape(tok_dev, heads_here, DH).astype(jnp.float32)).astype(
        jnp.bfloat16
    )
    key_norm = rms_rows(keys.reshape(tok_dev, heads_here, DH).astype(jnp.float32)).astype(
        jnp.bfloat16
    )
    gate_pre = jnp.einsum("thd,hdf->htf", key_norm, fast_one, preferred_element_type=jnp.float32)
    up_pre = jnp.einsum("thd,hdf->htf", key_norm, fast_three, preferred_element_type=jnp.float32)
    gate_sig = jax.nn.sigmoid(gate_pre)
    hidden_keys = (gate_pre * gate_sig * up_pre).astype(jnp.bfloat16)
    descent = (
        -step_size[:, :, None] * values.reshape(tok_dev, heads_here, DH).astype(jnp.float32)
    ).astype(jnp.bfloat16)
    grad_two = jnp.einsum("htf,thd->hfd", hidden_keys, descent, preferred_element_type=jnp.float32)
    back = jnp.einsum("thd,hfd->htf", descent, fast_two, preferred_element_type=jnp.float32)
    grad_gate = (back * up_pre * gate_sig * (1.0 + gate_pre * (1.0 - gate_sig))).astype(
        jnp.bfloat16
    )
    grad_up = (back * gate_pre * gate_sig).astype(jnp.bfloat16)
    grad_one = jnp.einsum("thd,htf->hdf", key_norm, grad_gate, preferred_element_type=jnp.float32)
    grad_three = jnp.einsum("thd,htf->hdf", key_norm, grad_up, preferred_element_type=jnp.float32)
    total_one, total_three, total_two = lax.psum((grad_one, grad_three, grad_two), "tok")
    new_one = (fast_one.astype(jnp.float32) - total_one).astype(jnp.bfloat16)
    new_three = (fast_three.astype(jnp.float32) - total_three).astype(jnp.bfloat16)
    new_two = (fast_two.astype(jnp.float32) - total_two).astype(jnp.bfloat16)
    gate_q = jnp.einsum("thd,hdf->htf", query_norm, new_one, preferred_element_type=jnp.float32)
    up_q = jnp.einsum("thd,hdf->htf", query_norm, new_three, preferred_element_type=jnp.float32)
    hidden_q = (gate_q * jax.nn.sigmoid(gate_q) * up_q).astype(jnp.bfloat16)
    fast_out = jnp.einsum(
        "htf,hfd->thd", hidden_q, new_two, preferred_element_type=jnp.float32
    ).reshape(tok_dev, local_width)
    mixed = (attended + fast_out).astype(jnp.bfloat16)
    mixed_full = lax.all_gather(mixed, "head", axis=1, tiled=True)
    projected = jnp.dot(
        mixed_full,
        lax.all_gather(out_proj, "tok", axis=0, tiled=True),
        preferred_element_type=jnp.float32,
    ).astype(jnp.bfloat16)
    tiles = projected.reshape(shard_count, tok_dev // shard_count, out_proj.shape[1])
    targets = evening.reshape(shard_count)
    match = (targets[None, :] == jnp.arange(shard_count, dtype=jnp.int32)[:, None]).astype(
        jnp.int32
    )
    order_index = jnp.argmax(match, axis=1)
    outgoing = tiles[order_index]
    arrived = lax.all_to_all(outgoing, "tok", split_axis=0, concat_axis=0, tiled=True)
    return arrived.reshape(tok_dev, out_proj.shape[1])


def solution(mesh):
    return jax.shard_map(
        local,
        mesh=mesh,
        in_specs=(
            P("tok", "head"),
            P("tok", "head"),
            P("tok", "head"),
            P("tok", "head"),
            P("head", None, None),
            P("head", None, None),
            P("head", None, None),
            P("tok", "head"),
            P(),
            P("tok", None),
        ),
        out_specs=P("tok", "head"),
        check_vma=False,
    )
```

profile of v0, /device:TPU:32, one launch (start us, length us, event | category | flops | bytes accessed | tf_op | source)
XLA Modules:
  0.0 387.9 jit_solution(13279123578200900547)
XLA Ops:
  6.5 1.5 fusion.12
  8.1 2.2 fusion.30
  10.4 0.8 fusion.28
  11.2 0.4 copy-done.1
  11.6 0.1 copy-done.4
  11.7 0.8 fusion.26
  12.5 2.1 convolution_bitcast_fusion
  14.6 2.3 convolution_bitcast_fusion.1
  16.9 2.1 convolution_bitcast_fusion.2
  19.0 0.7 all-gather.5.cloned.1.call-update
  19.8 1.5 pad_maximum_fusion.1
  21.3 3.8 collective-permute-start
  25.2 3.5 collective-permute-start.1
  28.7 0.1 copy.15
  28.8 0.1 reduce-window.8
  28.9 0.1 multiply_reduce_fusion
  29.1 0.2 convert_reduce_fusion.1
  29.3 0.3 fusion.14
  29.6 61.3 %collective-permute-done = bf16[2,1024,512]{2,1,0:T(8,128)(2,1)} collective-permute-done((bf16[2,1024,512]{2,1,0:T(8,128)(2,1)}, bf16[2,1024,512]{2,1,0:T(8,128)(2,1)}, u32[]{:S(2)}, u32[]{:S(2)}) %collective-permute-start) | collective-permute-done | bytes 2097184 | tf_op jit(solution)/shard_map/ppermute | solution.py:14
  90.9 4.1 %collective-permute-done.1 = bf16[2,1024,512]{2,1,0:T(8,128)(2,1)} collective-permute-done((bf16[2,1024,512]{2,1,0:T(8,128)(2,1)}, bf16[2,1024,512]{2,1,0:T(8,128)(2,1)}, u32[]{:S(2)}, u32[]{:S(2)}) %collective-permute-start.1) | collective-permute-done | bytes 2097184 | tf_op jit(solution)/shard_map/ppermute | solution.py:14
  95.1 3.5 pad_maximum_fusion
  98.6 3.1 slice_bitcast_fusion
  101.6 58.6 %while.10 = (s32[]{:T(128)}, f32[2,512,512]{1,0,2:T(2,128)}, s32[2]{0:T(128)S(1)}, bf16[3072,1,512]{2,0,1:T(8,128)(2,1)}, s32[1024]{0:T(1024)S(1)}, /*index=5*/s...) while((s32[]{:T(128)}, f32[2,512,512]{1,0,2:T(2,128)}, ...), condition=%wide.region_7.8_spmd, body=%wide.region_4.7_spmd.sunk | while | flops 2696150016 | bytes 39371012 | solution.py:87
  101.6 0.7 dynamic_slice.44
  103.2 3.6 fusion.51
  106.8 0.8 fusion.52
  107.6 1.1 copy-done.3
  108.7 1.8 fusion.53
  110.5 1.1 copy.23
  111.6 19.4 %dynamic_update_slice.5 = f32[2,512,512]{1,0,2:T(2,128)} dynamic-update-slice(f32[2,512,512]{1,0,2:T(2,128)} %get-tuple-element.145, f32[1,512,512]{1,0,2:T(1,128)S(1)} %copy.23, s32[]{:T(128)} %get-tuple-element.144, s32[]{:T(128)} %constant.16.clone.1..sunk, s32[]{:T(128)} %constant.16.clone.1..sunk) | dynamic-update-slice | bytes 2097156 | tf_op jit(solution)/shard_map/while/body/jit(dynamic_update_index_in_dim)/dynamic_update_slice | solution.py:87
  131.0 0.7 dynamic_slice.44
  132.5 3.6 fusion.51
  136.1 0.8 fusion.52
  136.9 1.1 copy-done.3
  138.0 1.8 fusion.53
  139.8 1.1 copy.23
  140.9 19.4 %dynamic_update_slice.5 = f32[2,512,512]{1,0,2:T(2,128)} dynamic-update-slice(f32[2,512,512]{1,0,2:T(2,128)} %get-tuple-element.145, f32[1,512,512]{1,0,2:T(1,128)S(1)} %copy.23, s32[]{:T(128)} %get-tuple-element.144, s32[]{:T(128)} %constant.16.clone.1..sunk, s32[]{:T(128)} %constant.16.clone.1..sunk) | dynamic-update-slice | bytes 2097156 | tf_op jit(solution)/shard_map/while/body/jit(dynamic_update_index_in_dim)/dynamic_update_slice | solution.py:87
  160.3 2.1 copy.21
  162.3 35.8 %all-reduce.3.cloned.1.call-done = (f32[1,512,512]{2,1,0:T(8,128)}, f32[1,512,512]{2,1,0:T(8,128)}, f32[1,512,512]{2,1,0:T(8,128)}) async-done(((f32[1,512,512]{2,1,0:T(8,128)}, f32[1,512,512]{2,1,0:T(8,128)}, f32[1,512,512]{2,1,0:T(8,128)}), (f32[1,512,512]{2,1,0:T(8,128)}, f32[1,512,512]{2,1,0:T(8,128)}, f32[1,512,512]{2,1,0:T(8,128)})) %all-reduce.3.cloned.1.call-update) | async-done | bytes 3145744 | tf_op jit(solution)/shard_map/psum | solution.py:109
  198.1 3.5 fusion.21
  201.6 5.2 %fusion.16 = bf16[1024,512]{0,1:T(8,128)(2,1)} fusion(f32[1024,512]{0,1:T(8,128)S(1)} %bitcast.81, f32[1024,512]{1,0:T(8,128)} %fusion.21, f32[1,512,512]{2,1,0:T(8,128)} %get-tuple-element.70, bf16[1,512,512]{2,1,0:T(8,128)(2,1)} %param.18, f32[1,512,512]{2,1,0:T(8,128)} %get-tuple-element.71, bf16[1,512,512]{2,1,0:T(8,128)(2,1)} %param.17, ...), kind=kOutput, calls=%fused_computation.27 | convolution fusion | flops 1081081856 | bytes 9441280 | tf_op jit(solution)/shard_map/htf,hfd->thd/dot_general | solution.py:116
  206.8 0.9 iota_reduce_fusion
  207.7 73.3 %all-gather.5.cloned.1.call-done = bf16[4096,512]{1,0:T(8,128)(2,1)} async-done(((bf16[128,512]{1,0:T(8,128)(2,1)}), bf16[4096,512]{1,0:T(8,128)(2,1)}) %all-gather.5.cloned.1.call-update) | async-done | bytes 4194320 | tf_op jit(solution)/shard_map/all_gather | solution.py:123
  281.0 51.2 %all-gather.3.cloned.1.call-done = bf16[1024,4096]{0,1:T(8,128)(2,1)} async-done(((bf16[1024,512]{0,1:T(8,128)(2,1)}), bf16[1024,4096]{0,1:T(8,128)(2,1)}) %all-gather.3.cloned.1.call-update) | async-done | bytes 8388624 | tf_op jit(solution)/shard_map/all_gather | solution.py:120
  332.2 9.1 %convolution_convert_fusion = bf16[1024,512]{1,0:T(8,128)(2,1)S(1)} fusion(bf16[1024,4096]{0,1:T(8,128)(2,1)} %all-gather.3.cloned.1.call-done, bf16[4096,512]{1,0:T(8,128)(2,1)} %all-gather.5.cloned.1.call-done), kind=kOutput, calls=%fused_computation.34 | convolution fusion | flops 4295491584 | bytes 13631488 | tf_op jit(solution)/shard_map/dot_general | solution.py:121
  341.2 0.6 gather_fusion
  341.9 38.6 %all_to_all.5 = bf16[32,32,512]{2,1,0:T(8,128)(2,1)S(1)} all-to-all(bf16[32,32,512]{2,1,0:T(8,128)(2,1)S(1)} %gather_fusion), channel_id=1, replica_groups=mesh['head'=8,'tok'=32] {'tok'}, dimensions={0} | all-to-all | bytes 2097152 | tf_op jit(solution)/shard_map/all_to_all | solution.py:133
  380.4 1.0 copy.35
  (38 shorter events, 0.5 us)
Async XLA Ops:
  6.5 191.6 %all-reduce.3.cloned.1.call-start = ((), (), s32[]{:S(2)}) async-start(), calls=%async_computation.3 | async-start | bytes 6291456 | tf_op jit(solution)/shard_map/psum | solution.py:109
  8.0 2.3 copy-start
  8.1 2.3 copy-start.5
  10.3 0.8 copy-start.6
  10.3 1.2 copy-start.1
  10.4 1.4 copy-start.4
  19.0 262.0 %all-gather.5.cloned.1.call-start = ((), (), s32[]{:S(2)}) async-start(), calls=%async_computation.2 | async-start | bytes 4325376 | tf_op jit(solution)/shard_map/all_gather | solution.py:123
  19.7 312.4 %all-gather.3.cloned.1.call-start = ((), (), s32[]{:S(2)}) async-start(), calls=%async_computation.1 | async-start | bytes 9437184 | tf_op jit(solution)/shard_map/all_gather | solution.py:120
  19.8 8.9 %copy-start.7 = (s32[64]{0:T(128)S(1)}, s32[64]{0:T(128)}, u32[]{:S(2)}) copy-start(s32[64]{0:T(128)} %param.20) | copy-start | bytes 772
  19.8 9.5 %copy-start.2 = (bf16[1024,512]{1,0:T(8,128)(2,1)S(1)}, bf16[1024,512]{1,0:T(8,128)(2,1)}, u32[]{:S(2)}) copy-start(bf16[1024,512]{1,0:T(8,128)(2,1)} %param.12) | copy-start | bytes 3145732
  21.3 69.6 %collective-permute-start = (bf16[2,1024,512]{2,1,0:T(8,128)(2,1)}, bf16[2,1024,512]{2,1,0:T(8,128)(2,1)}, u32[]{:S(2)}, u32[]{:S(2)}) collective-permute-start(bf16[2,1024,512]{2,1,0:T(8,128)(2,1)} %pad_maximum_fusion.1), channel_id=1, source_target_pairs={{0,1},{1,2},{2,3},{3,4},{4,5},{5,6},{6,7},{7,8},{8,9},{9,10},{10,1... | collective-permute-start | bytes 6291464 | tf_op jit(solution)/shard_map/ppermute | solution.py:14
  25.2 69.9 %collective-permute-start.1 = (bf16[2,1024,512]{2,1,0:T(8,128)(2,1)}, bf16[2,1024,512]{2,1,0:T(8,128)(2,1)}, u32[]{:S(2)}, u32[]{:S(2)}) collective-permute-start(bf16[2,1024,512]{2,1,0:T(8,128)(2,1)} %pad_maximum_fusion.1), channel_id=1, source_target_pairs={{1,0},{2,1},{3,2},{4,3},{5,4},{6,5},{7,6},{8,7},{9,8},{10,9},{11,1... | collective-permute-start | bytes 6291464 | tf_op jit(solution)/shard_map/ppermute | solution.py:14
  106.8 1.9 copy-start.3
  136.1 1.9 copy-start.3
  201.6 5.2 %copy-start.8 = (s32[1,32]{1,0:T(1,128)S(1)}, s32[1,32]{1,0:T(1,128)}, u32[]{:S(2)}) copy-start(s32[1,32]{1,0:T(1,128)} %param.21) | copy-start | bytes 388
Sparse Core Ops, SparseCore 0:
  19.1 178.9 all-reduce.2
  200.7 80.2 all-gather.4
  282.8 49.2 all-gather.2
where the time goes:
time: 391 us; the launch traced here: 388 us
  waiting for transfers between devices  226 us (58%)
  local copies, waits for them, and re-layouts  52.1 us (13%)
  matrix products  38.8 us (10%)
  blocking collectives  38.6 us (10%)
  between operations  13.4 us (3%)
  other arithmetic  9.8 us (3%)
  starting transfers between devices  7.41 us (2%)
    all_gather x1, waiting for transfers between devices, local(): lax.all_gather(out_proj, 'tok', axis=0, tiled=True)  73.3 us
    ppermute x2, waiting for transfers between devices, from_behind(): lax.ppermute(value, axis, [(source, source + steps) for source in range(l...  65.5 us
    all_gather x1, waiting for transfers between devices, local(): mixed_full = lax.all_gather(mixed, 'head', axis=1, tiled=True)  51.2 us
    dynamic_update_slice x4, local copies, waits for them, and re-layouts, local(): lax.map(attend, jnp.arange(n_blocks, dtype=jnp.int32))  41 us
    all_to_all x1, blocking collectives, local(): lax.all_to_all(outgoing, 'tok', split_axis=0, concat_axis=0, tiled=True)  38.6 us
    psum x1, waiting for transfers between devices, local(): lax.psum((grad_one, grad_three, grad_two), 'tok')  35.8 us
    dot_general x1, matrix products, local(): jnp.dot(mixed_full, lax.all_gather(out_proj, 'tok', axis=0, tiled=True),...  9.08 us
  transfers between devices with their start and end apart: 5, of which 5 were waited for; matrix products, arithmetic and copies ran while one was open for 19% of the time, Pallas kernels for 0%

commit v1 on v0

--- a/solution.py
+++ b/solution.py
@@ -117,7 +117,9 @@
         "htf,hfd->thd", hidden_q, new_two, preferred_element_type=jnp.float32
     ).reshape(tok_dev, local_width)
     mixed = (attended + fast_out).astype(jnp.bfloat16)
-    mixed_full = lax.all_gather(mixed, "head", axis=1, tiled=True)
+    mixed_full = jnp.concatenate(
+        lax.all_to_all(jnp.stack([mixed] * lax.axis_size("head")), "head", 0, 0), axis=1
+    )
     projected = jnp.dot(
         mixed_full,
         lax.all_gather(out_proj, "tok", axis=0, tiled=True),

time: 391 us -> 368 us (0.941)
  waiting for transfers between devices: 226 us -> 195 us
  local copies, waits for them, and re-layouts: 52.1 us -> 57.4 us
  starting transfers between devices: 7.41 us -> 12.7 us
    all_gather x1 -> x0, waiting for transfers between devices: 51.2 us -> none  [local(): mixed_full = lax.all_gather(mixed, 'head', axis=1, tiled=True)]
    all_to_all x0 -> x1, waiting for transfers between devices: none -> 30.9 us  [local(): lax.all_to_all(jnp.stack([mixed] * lax.axis_size('head')), 'head', 0, 0)]
    all_gather x1, waiting for transfers between devices: 73.3 us -> 62.8 us  [local(): lax.all_gather(out_proj, 'tok', axis=0, tiled=True)]
    another operation x1 -> x2, local copies, waits for them, and re-layouts: 0.1 us -> 5.61 us  [the longest x1 5.52 us: local(): jnp.stack([mixed] * lax.axis_size('head'))]
    all_to_all x0 -> x1, starting transfers between devices: none -> 5.31 us  [local(): lax.all_to_all(jnp.stack([mixed] * lax.axis_size('head')), 'head', 0, 0)]
  transfers between devices with their start and end apart: 5 -> 5, of which waited for: 5 -> 5; matrix products, arithmetic and copies ran while one was open for 19% -> 22% of each run, Pallas kernels for 0% -> 0%
where the time goes in v1:
time: 368 us; the launch traced here: 364 us
  waiting for transfers between devices  195 us (53%)
  local copies, waits for them, and re-layouts  57.4 us (16%)
  matrix products  38.8 us (11%)
  blocking collectives  35.6 us (10%)
  between operations  13.7 us (4%)
  starting transfers between devices  12.7 us (3%)
  other arithmetic  9.56 us (3%)
    ppermute x2, waiting for transfers between devices, from_behind(): lax.ppermute(value, axis, [(source, source + steps) for source in range(l...  65.4 us
    all_gather x1, waiting for transfers between devices, local(): lax.all_gather(out_proj, 'tok', axis=0, tiled=True)  62.8 us
    dynamic_update_slice x4, local copies, waits for them, and re-layouts, local(): lax.map(attend, jnp.arange(n_blocks, dtype=jnp.int32))  41 us
    psum x1, waiting for transfers between devices, local(): lax.psum((grad_one, grad_three, grad_two), 'tok')  36.3 us
    all_to_all x1, blocking collectives, local(): lax.all_to_all(outgoing, 'tok', split_axis=0, concat_axis=0, tiled=True)  35.6 us
    all_to_all x1, waiting for transfers between devices, local(): lax.all_to_all(jnp.stack([mixed] * lax.axis_size('head')), 'head', 0, 0)  30.9 us
    dot_general x1, matrix products, local(): jnp.dot(mixed_full, lax.all_gather(out_proj, 'tok', axis=0, tiled=True),...  9.09 us
  transfers between devices with their start and end apart: 5, of which 5 were waited for; matrix products, arithmetic and copies ran while one was open for 22% of the time, Pallas kernels for 0%

profile of v1, /device:TPU:32, one launch (start us, length us, event | category | flops | bytes accessed | tf_op | source)
XLA Modules:
  0.0 364.4 jit_solution(6910458415063587635)
XLA Ops:
  6.5 1.5 fusion.12
  8.1 2.2 fusion.30
  10.4 0.8 fusion.28
  11.2 0.4 copy-done.1
  11.6 0.1 copy-done.4
  11.7 0.8 fusion.26
  12.5 2.1 convolution_bitcast_fusion
  14.6 2.3 convolution_bitcast_fusion.1
  16.9 2.1 convolution_bitcast_fusion.2
  19.1 1.5 pad_maximum_fusion.1
  20.6 3.8 %collective-permute-start = (bf16[2,1024,512]{2,1,0:T(8,128)(2,1)}, bf16[2,1024,512]{2,1,0:T(8,128)(2,1)}, u32[]{:S(2)}, u32[]{:S(2)}) collective-permute-start(bf16[2,1024,512]{2,1,0:T(8,128)(2,1)} %pad_maximum_fusion.1), channel_id=1, source_target_pairs={{0,1},{1,2},{2,3},{3,4},{4,5},{5,6},{6,7},{7,8},{8,9},{9,10},{10,1... | collective-permute-start | bytes 6291464 | tf_op jit(solution)/shard_map/ppermute | solution.py:14
  24.4 3.5 collective-permute-start.1
  28.0 0.1 copy.16
  28.2 0.1 multiply_reduce_fusion
  28.3 0.2 convert_reduce_fusion.1
  28.6 0.3 fusion.14
  28.9 61.3 %collective-permute-done = bf16[2,1024,512]{2,1,0:T(8,128)(2,1)} collective-permute-done((bf16[2,1024,512]{2,1,0:T(8,128)(2,1)}, bf16[2,1024,512]{2,1,0:T(8,128)(2,1)}, u32[]{:S(2)}, u32[]{:S(2)}) %collective-permute-start) | collective-permute-done | bytes 2097184 | tf_op jit(solution)/shard_map/ppermute | solution.py:14
  90.2 4.1 %collective-permute-done.1 = bf16[2,1024,512]{2,1,0:T(8,128)(2,1)} collective-permute-done((bf16[2,1024,512]{2,1,0:T(8,128)(2,1)}, bf16[2,1024,512]{2,1,0:T(8,128)(2,1)}, u32[]{:S(2)}, u32[]{:S(2)}) %collective-permute-start.1) | collective-permute-done | bytes 2097184 | tf_op jit(solution)/shard_map/ppermute | solution.py:14
  94.3 3.5 pad_maximum_fusion
  97.8 3.1 slice_bitcast_fusion
  100.9 58.2 %while.10 = (s32[]{:T(128)}, f32[2,512,512]{1,0,2:T(2,128)}, s32[2]{0:T(128)S(1)}, bf16[3072,1,512]{2,0,1:T(8,128)(2,1)}, s32[1024]{0:T(1024)S(1)}, /*index=5*/s...) while((s32[]{:T(128)}, f32[2,512,512]{1,0,2:T(2,128)}, ...), condition=%wide.region_7.8_spmd, body=%wide.region_4.7_spmd.sunk | while | flops 2696150016 | bytes 39371012 | solution.py:87
  100.9 0.6 dynamic_slice.44
  102.2 3.6 fusion.51
  105.8 0.8 fusion.52
  106.6 1.1 copy-done.3
  107.7 1.8 fusion.53
  109.5 1.1 copy.24
  110.6 19.4 %dynamic_update_slice.5 = f32[2,512,512]{1,0,2:T(2,128)} dynamic-update-slice(f32[2,512,512]{1,0,2:T(2,128)} %get-tuple-element.145, f32[1,512,512]{1,0,2:T(1,128)S(1)} %copy.24, s32[]{:T(128)} %get-tuple-element.144, s32[]{:T(128)} %constant.16.clone.1..sunk, s32[]{:T(128)} %constant.16.clone.1..sunk) | dynamic-update-slice | bytes 2097156 | tf_op jit(solution)/shard_map/while/body/jit(dynamic_update_index_in_dim)/dynamic_update_slice | solution.py:87
  130.0 0.6 dynamic_slice.44
  131.2 3.6 fusion.51
  134.9 0.8 fusion.52
  135.7 1.1 copy-done.3
  136.8 1.8 fusion.53
  138.6 1.1 copy.24
  139.6 19.4 %dynamic_update_slice.5 = f32[2,512,512]{1,0,2:T(2,128)} dynamic-update-slice(f32[2,512,512]{1,0,2:T(2,128)} %get-tuple-element.145, f32[1,512,512]{1,0,2:T(1,128)S(1)} %copy.24, s32[]{:T(128)} %get-tuple-element.144, s32[]{:T(128)} %constant.16.clone.1..sunk, s32[]{:T(128)} %constant.16.clone.1..sunk) | dynamic-update-slice | bytes 2097156 | tf_op jit(solution)/shard_map/while/body/jit(dynamic_update_index_in_dim)/dynamic_update_slice | solution.py:87
  159.1 2.1 copy.22
  161.1 36.3 %all-reduce.3.cloned.1.call-done = (f32[1,512,512]{2,1,0:T(8,128)}, f32[1,512,512]{2,1,0:T(8,128)}, f32[1,512,512]{2,1,0:T(8,128)}) async-done(((f32[1,512,512]{2,1,0:T(8,128)}, f32[1,512,512]{2,1,0:T(8,128)}, f32[1,512,512]{2,1,0:T(8,128)}), (f32[1,512,512]{2,1,0:T(8,128)}, f32[1,512,512]{2,1,0:T(8,128)}, f32[1,512,512]{2,1,0:T(8,128)})) %all-reduce.3.cloned.1.call-update) | async-done | bytes 3145744 | tf_op jit(solution)/shard_map/psum | solution.py:109
  197.4 3.5 fusion.21
  200.9 5.2 %fusion.16 = bf16[1024,512]{0,1:T(8,128)(2,1)} fusion(f32[1024,512]{0,1:T(8,128)S(1)} %bitcast.84, f32[1024,512]{1,0:T(8,128)} %fusion.21, f32[1,512,512]{2,1,0:T(8,128)} %get-tuple-element.70, bf16[1,512,512]{2,1,0:T(8,128)(2,1)} %param.18, f32[1,512,512]{2,1,0:T(8,128)} %get-tuple-element.71, bf16[1,512,512]{2,1,0:T(8,128)(2,1)} %param.17, ...), kind=kOutput, calls=%fused_computation.27 | convolution fusion | flops 1081081856 | bytes 9441280 | tf_op jit(solution)/shard_map/htf,hfd->thd/dot_general | solution.py:116
  206.0 5.5 %stack.11 = bf16[8,1024,512]{1,2,0:T(8,128)(2,1)} broadcast(bf16[1024,512]{0,1:T(8,128)(2,1)} %fusion.16), dimensions={1,2} | broadcast | bytes 9437184 | tf_op jit(solution)/shard_map/stack | solution.py:121
  211.5 5.3 %all-to-all-start = ((bf16[8,1024,512]{1,2,0:T(8,128)(2,1)}), bf16[8,1024,512]{1,2,0:T(8,128)(2,1)}, u32[]{:S(2)}, u32[]{:S(2)}) async-start(bf16[8,1024,512]{1,2,0:T(8,128)(2,1)} %stack.11), calls=%async_computation | async-start | bytes 16777216 | tf_op jit(solution)/shard_map/all_to_all | solution.py:121
  216.9 0.6 iota_reduce_fusion
  217.5 62.8 %all-gather.2.cloned.1.call-done = bf16[4096,512]{1,0:T(8,128)(2,1)} async-done(((bf16[128,512]{1,0:T(8,128)(2,1)}), bf16[4096,512]{1,0:T(8,128)(2,1)}) %all-gather.2.cloned.1.call-update) | async-done | bytes 4194320 | tf_op jit(solution)/shard_map/all_gather | solution.py:125
  280.3 30.9 %all-to-all-done = bf16[8,1024,512]{1,2,0:T(8,128)(2,1)} async-done(((bf16[8,1024,512]{1,2,0:T(8,128)(2,1)}), bf16[8,1024,512]{1,2,0:T(8,128)(2,1)}, u32[]{:S(2)}, u32[]{:S(2)}) %all-to-all-start) | async-done | bytes 8388640 | tf_op jit(solution)/shard_map/all_to_all | solution.py:121
  311.2 9.1 %convolution_convert_fusion = bf16[1024,512]{1,0:T(8,128)(2,1)S(1)} fusion(bf16[1024,4096]{0,1:T(8,128)(2,1)} %bitcast.25, bf16[4096,512]{1,0:T(8,128)(2,1)} %all-gather.2.cloned.1.call-done), kind=kOutput, calls=%fused_computation.34 | convolution fusion | flops 4295491584 | bytes 13631488 | tf_op jit(solution)/shard_map/dot_general | solution.py:123
  320.3 0.6 gather_fusion
  320.9 35.6 %all_to_all.10 = bf16[32,32,512]{2,1,0:T(8,128)(2,1)S(1)} all-to-all(bf16[32,32,512]{2,1,0:T(8,128)(2,1)S(1)} %gather_fusion), channel_id=1, replica_groups=mesh['head'=8,'tok'=32] {'tok'}, dimensions={0} | all-to-all | bytes 2097152 | tf_op jit(solution)/shard_map/all_to_all | solution.py:135
  356.6 1.0 copy.36
  (38 shorter events, 0.6 us)
Async XLA Ops:
  6.5 190.9 %all-reduce.3.cloned.1.call-start = ((), (), s32[]{:S(2)}) async-start(), calls=%async_computation.3 | async-start | bytes 6291456 | tf_op jit(solution)/shard_map/psum | solution.py:109
  8.0 2.3 copy-start
  8.1 2.3 copy-start.5
  10.3 0.8 copy-start.6
  10.3 1.2 copy-start.1
  10.4 1.4 copy-start.4
  19.0 261.3 %all-gather.2.cloned.1.call-start = ((), (), s32[]{:S(2)}) async-start(), calls=%async_computation.2 | async-start | bytes 4325376 | tf_op jit(solution)/shard_map/all_gather | solution.py:125
  19.1 9.0 %copy-start.7 = (s32[64]{0:T(128)S(1)}, s32[64]{0:T(128)}, u32[]{:S(2)}) copy-start(s32[64]{0:T(128)} %param.20) | copy-start | bytes 772
  19.1 9.5 %copy-start.2 = (bf16[1024,512]{1,0:T(8,128)(2,1)S(1)}, bf16[1024,512]{1,0:T(8,128)(2,1)}, u32[]{:S(2)}) copy-start(bf16[1024,512]{1,0:T(8,128)(2,1)} %param.12) | copy-start | bytes 3145732
  20.6 69.6 %collective-permute-start = (bf16[2,1024,512]{2,1,0:T(8,128)(2,1)}, bf16[2,1024,512]{2,1,0:T(8,128)(2,1)}, u32[]{:S(2)}, u32[]{:S(2)}) collective-permute-start(bf16[2,1024,512]{2,1,0:T(8,128)(2,1)} %pad_maximum_fusion.1), channel_id=1, source_target_pairs={{0,1},{1,2},{2,3},{3,4},{4,5},{5,6},{6,7},{7,8},{8,9},{9,10},{10,1... | collective-permute-start | bytes 6291464 | tf_op jit(solution)/shard_map/ppermute | solution.py:14
  24.4 69.8 %collective-permute-start.1 = (bf16[2,1024,512]{2,1,0:T(8,128)(2,1)}, bf16[2,1024,512]{2,1,0:T(8,128)(2,1)}, u32[]{:S(2)}, u32[]{:S(2)}) collective-permute-start(bf16[2,1024,512]{2,1,0:T(8,128)(2,1)} %pad_maximum_fusion.1), channel_id=1, source_target_pairs={{1,0},{2,1},{3,2},{4,3},{5,4},{6,5},{7,6},{8,7},{9,8},{10,9},{11,1... | collective-permute-start | bytes 6291464 | tf_op jit(solution)/shard_map/ppermute | solution.py:14
  105.8 1.9 copy-start.3
  134.9 1.9 copy-start.3
  211.5 5.3 %copy-start.8 = (s32[1,32]{1,0:T(1,128)S(1)}, s32[1,32]{1,0:T(1,128)}, u32[]{:S(2)}) copy-start(s32[1,32]{1,0:T(1,128)} %param.21) | copy-start | bytes 388
  211.5 99.7 %all-to-all-start = ((bf16[8,1024,512]{1,2,0:T(8,128)(2,1)}), bf16[8,1024,512]{1,2,0:T(8,128)(2,1)}, u32[]{:S(2)}, u32[]{:S(2)}) async-start(bf16[8,1024,512]{1,2,0:T(8,128)(2,1)} %stack.11), calls=%async_computation | async-start | bytes 16777216 | tf_op jit(solution)/shard_map/all_to_all | solution.py:121
Sparse Core Ops, SparseCore 0:
  19.1 178.2 all-reduce.2
  200.0 80.2 all-gather.1
